TPU v7x, 512 devices: a whole 4x4x16 slice. The times are simulated.
512 devices in a mesh: dp: 4 (over y), expert: 32 (over z, core), tensor: 4 (over x).
Axes of the slice: x: 4, y: 4, z: 16, core: 2. Of those that a mesh axis runs over, the one named last changes fastest.
Arguments:
- tokens: bfloat16 [16384, 2048], P(('dp', 'expert')), may hold values from -6 to 6
- cotangent: bfloat16 [16384, 2048], P(('dp', 'expert')), may hold values from -6 to 6
- expert_ids: int32 [16384, 1], P(('dp', 'expert')), may hold values from 0 to 31; in each aligned block of 128 rows (0 to 127, 128 to 255, ...) at most 8 rows name the same one
- gate_weight: bfloat16 [32, 2048, 1408], P('expert', 'dp', 'tensor'), may hold values from -0.125 to 0.125
- up_weight: bfloat16 [32, 2048, 1408], P('expert', 'dp', 'tensor'), may hold values from -0.125 to 0.125
- down_weight: bfloat16 [32, 2048, 1408], P('expert', 'dp', 'tensor'), may hold values from -0.15625 to 0.15625
Outputs:
- grad_tokens: bfloat16 [16384, 2048], P(('dp', 'expert'), 'tensor')
- grad_gate: bfloat16 [32, 2048, 1408], P('expert', 'dp', 'tensor')
- grad_up: bfloat16 [32, 2048, 1408], P('expert', 'dp', 'tensor')
Inputs may be any that keep to these rules, and one draw needn't show every extreme that they name: `expert_ids`: among the 128 tokens of one block no expert id occurs more than 8 times, and in every draw some block holds some id exactly 8 times.
All inputs are finite; a program needn't handle non-finite values.
Results may differ from a plain program's by a relative error of at most 0.013.
Values may be sent and summed in bfloat16 or wider, within the bound.
A program may use at most 64 MiB of HBM per device.

v0:
```python
import jax
import jax.numpy as jnp
from jax import lax
from jax.sharding import PartitionSpec as P

CAP = 8


def bucket_matrix(expert_ids, expert_count, capacity):
    chosen = expert_ids[:, 0]
    columns = jnp.arange(expert_count, dtype=jnp.int32)
    onehot = (chosen[:, None] == columns[None, :]).astype(jnp.int32)
    earlier = jnp.cumsum(onehot, axis=0) - onehot
    position = jnp.sum(earlier * onehot, axis=1)
    target = chosen * capacity + position
    slot_rows = jnp.arange(expert_count * capacity, dtype=jnp.int32)
    return (slot_rows[:, None] == target[None, :]).astype(jnp.bfloat16)


def on_device(tokens, cotangent, expert_ids, gate_weight, up_weight, down_weight):
    owners = lax.axis_size("expert")
    shards = lax.axis_size("tensor")
    features = tokens.shape[1]
    part = features // shards
    local_experts = gate_weight.shape[0]
    expert_count = local_experts * owners
    slot_count = owners * CAP
    placer = bucket_matrix(expert_ids, expert_count, CAP)
    gate_full, down_full, up_full = (
        lax.all_gather(w, "dp", axis=1, tiled=True)[0]
        for w in (gate_weight, down_weight, up_weight)
    )
    start = lax.axis_index("tensor") * part
    mine = jnp.concatenate(
        [lax.dynamic_slice_in_dim(a, start, part, axis=1) for a in (tokens, cotangent)], axis=1
    )
    packed = jnp.dot(placer, mine, preferred_element_type=jnp.float32).astype(jnp.bfloat16)
    arrived = lax.all_to_all(
        packed.reshape(owners, CAP, 2 * part), "expert", split_axis=0, concat_axis=0, tiled=True
    ).reshape(slot_count, 2 * part)
    whole = lax.all_gather(arrived, "tensor", axis=0, tiled=False)
    inputs = jnp.concatenate([whole[t, :, :part] for t in range(shards)], axis=1)
    grads_in = jnp.concatenate([whole[t, :, part:] for t in range(shards)], axis=1)
    gate_act = jnp.dot(inputs, gate_full, preferred_element_type=jnp.float32)
    hidden_grad = jnp.dot(grads_in, down_full, preferred_element_type=jnp.float32)
    up_act = jnp.dot(inputs, up_full, preferred_element_type=jnp.float32)
    sigmoid_gate = jax.nn.sigmoid(gate_act)
    up_grad = (hidden_grad * gate_act * sigmoid_gate).astype(jnp.bfloat16)
    gate_grad = (
        hidden_grad * up_act * sigmoid_gate * (1.0 + gate_act * (1.0 - sigmoid_gate))
    ).astype(jnp.bfloat16)
    contract = (((1,), (1,)), ((), ()))
    partial_value = lax.dot_general(
        gate_grad, gate_full, contract, preferred_element_type=jnp.float32
    )
    partial_value = partial_value + lax.dot_general(
        up_grad, up_full, contract, preferred_element_type=jnp.float32
    )
    rows = (((0,), (0,)), ((), ()))
    gate_term = lax.dot_general(inputs, gate_grad, rows, preferred_element_type=jnp.float32)
    up_term = lax.dot_general(inputs, up_grad, rows, preferred_element_type=jnp.float32)
    summed = lax.psum_scatter(
        partial_value.astype(jnp.bfloat16), "tensor", scatter_dimension=1, tiled=True
    )
    grad_gate, grad_up = (
        lax.psum_scatter(term.astype(jnp.bfloat16), "dp", scatter_dimension=0, tiled=True)[None]
        for term in (gate_term, up_term)
    )
    returned = lax.all_to_all(
        summed.reshape(owners, CAP, part), "expert", split_axis=0, concat_axis=0, tiled=True
    ).reshape(slot_count, part)
    per_token = lax.dot_general(placer, returned, rows, preferred_element_type=jnp.float32)
    return (per_token.astype(jnp.bfloat16), grad_gate, grad_up)


def solution(mesh):
    placed = (
        P(("dp", "expert"), None),
        P(("dp", "expert"), None),
        P(("dp", "expert"), None),
        P("expert", "dp", "tensor"),
        P("expert", "dp", "tensor"),
        P("expert", "dp", "tensor"),
    )
    return jax.shard_map(
        on_device,
        mesh=mesh,
        in_specs=placed,
        out_specs=(
            P(("dp", "expert"), "tensor"),
            P("expert", "dp", "tensor"),
            P("expert", "dp", "tensor"),
        ),
        check_vma=False,
    )
```

profile of v0, /device:TPU:4, one launch (start us, length us, event | category | flops | bytes accessed | tf_op | source)
XLA Modules:
  0.0 313.7 jit_solution(8685269563842167810)
XLA Ops:
  7.2 0.0 all-gather.5.cloned.1.call-start
  7.2 0.7 fusion.36
  8.0 0.2 reduce_window_sum.11
  8.1 0.8 select_reduce_fusion
  9.0 0.7 multiply_add_fusion
  9.6 1.0 constant_dynamic-slice_fusion
  10.6 0.3 fusion.10
  10.9 49.1 %all_to_all.10 = bf16[32,8,1024]{2,1,0:T(8,128)(2,1)} all-to-all(bf16[32,8,1024]{2,1,0:T(8,128)(2,1)S(1)} %fusion.10), channel_id=1, replica_groups=mesh['dp'=4,'expert'=32,'tensor'=4] {'expert'}, dimensions={0} | all-to-all | bytes 1048576 | tf_op jit(solution)/shard_map/all_to_all | solution.py:38
  60.1 0.0 all-gather.5.cloned.1.call-update
  60.1 0.0 all-gather.11.cloned.1.call-start
  60.1 0.7 all-gather.11.cloned.1.call-update
  60.8 0.0 all-gather.7.cloned.1.call-start
  60.9 0.7 all-gather.7.cloned.1.call-update
  61.6 0.0 all-gather.9.cloned.1.call-start
  61.6 0.5 all-gather.9.cloned.1.call-update
  62.1 0.0 reduce-scatter.4.cloned.1.call-start
  62.2 26.8 %all-gather.5.cloned.1.call-done = bf16[4,256,1024]{2,1,0:T(8,128)(2,1)} async-done(((bf16[1,256,1024]{2,1,0:T(8,128)(2,1)}), bf16[4,256,1024]{2,1,0:T(8,128)(2,1)}) %all-gather.5.cloned.1.call-update) | async-done | bytes 2097168 | tf_op jit(solution)/shard_map/all_gather | solution.py:41
  89.0 1.7 slice_bitcast_fusion.3
  90.7 34.9 %all-gather.11.cloned.1.call-done = bf16[1,2048,352]{1,2,0:T(8,128)(2,1)} async-done(((bf16[1,512,352]{1,2,0:T(8,128)(2,1)}), bf16[1,2048,352]{1,2,0:T(8,128)(2,1)}) %all-gather.11.cloned.1.call-update) | async-done | bytes 1441808 | tf_op jit(solution)/shard_map/all_gather | solution.py:30
  125.6 1.9 fusion.3
  127.5 33.9 %all-gather.7.cloned.1.call-done = bf16[1,2048,352]{1,2,0:T(8,128)(2,1)} async-done(((bf16[1,512,352]{1,2,0:T(8,128)(2,1)}), bf16[1,2048,352]{1,2,0:T(8,128)(2,1)}) %all-gather.7.cloned.1.call-update) | async-done | bytes 1441808 | tf_op jit(solution)/shard_map/all_gather | solution.py:30
  161.5 1.9 multiply_convert_fusion
  163.4 33.8 %all-gather.9.cloned.1.call-done = bf16[1,2048,352]{1,2,0:T(8,128)(2,1)} async-done(((bf16[1,512,352]{1,2,0:T(8,128)(2,1)}), bf16[1,2048,352]{1,2,0:T(8,128)(2,1)}) %all-gather.9.cloned.1.call-update) | async-done | bytes 1441808 | tf_op jit(solution)/shard_map/all_gather | solution.py:30
  197.2 0.0 copy-start
  197.2 2.1 fusion.20
  199.3 0.0 copy-done
  199.3 0.0 copy-start.1
  199.3 0.7 fusion.1
  200.0 0.6 copy-done.1
  200.7 1.7 fusion
  202.4 0.0 reduce-scatter.4.cloned.1.call-update
  202.4 0.0 reduce-scatter.8.cloned.1.call-start
  202.4 1.6 convolution_convert_fusion
  204.1 0.0 reduce-scatter.8.cloned.1.call-update
  204.1 0.0 reduce-scatter.6.cloned.1.call-start
  204.2 1.7 convolution_convert_fusion.1
  205.8 0.0 reduce-scatter.6.cloned.1.call-update
  205.9 26.9 %reduce-scatter.4.cloned.1.call-done = bf16[256,512]{1,0:T(8,128)(2,1)} async-done(((bf16[256,2048]{1,0:T(8,128)(2,1)}), bf16[256,512]{1,0:T(8,128)(2,1)}) %reduce-scatter.4.cloned.1.call-update) | async-done | bytes 262160 | tf_op jit(solution)/shard_map/reduce_scatter | solution.py:62
  232.8 35.4 %all_to_all.11 = bf16[32,8,512]{2,1,0:T(8,128)(2,1)S(1)} all-to-all(bf16[32,8,512]{2,1,0:T(8,128)(2,1)} %bitcast.55), channel_id=1, replica_groups=mesh['dp'=4,'expert'=32,'tensor'=4] {'expert'}, dimensions={0} | all-to-all | bytes 524288 | tf_op jit(solution)/shard_map/all_to_all | solution.py:69
  268.2 0.9 convolution_convert_fusion.3
  269.0 1.5 reduce-scatter.8.cloned.1.call-done
  270.5 36.3 %reduce-scatter.6.cloned.1.call-done = bf16[512,352]{0,1:T(8,128)(2,1)} async-done(((bf16[2048,352]{0,1:T(8,128)(2,1)}), bf16[512,352]{0,1:T(8,128)(2,1)}) %reduce-scatter.6.cloned.1.call-update) | async-done | bytes 360464 | tf_op jit(solution)/shard_map/reduce_scatter | solution.py:66
Async XLA Ops:
  7.2 81.8 %all-gather.5.cloned.1.call-start = ((), (), s32[]{:S(2)}) async-start(), calls=%async_computation.5 | async-start | bytes 2621440 | tf_op jit(solution)/shard_map/all_gather | solution.py:41
  60.1 65.5 %all-gather.11.cloned.1.call-start = ((), (), s32[]{:S(2)}) async-start(), calls=%async_computation.8 | async-start | bytes 1802240 | tf_op jit(solution)/shard_map/all_gather | solution.py:30
  60.8 100.6 %all-gather.7.cloned.1.call-start = ((), (), s32[]{:S(2)}) async-start(), calls=%async_computation.6 | async-start | bytes 1802240 | tf_op jit(solution)/shard_map/all_gather | solution.py:30
  61.6 135.6 %all-gather.9.cloned.1.call-start = ((), (), s32[]{:S(2)}) async-start(), calls=%async_computation.7 | async-start | bytes 1802240 | tf_op jit(solution)/shard_map/all_gather | solution.py:30
  62.1 170.6 %reduce-scatter.4.cloned.1.call-start = ((), (), s32[]{:S(2)}) async-start(), calls=%async_computation.9 | async-start | bytes 1310720 | tf_op jit(solution)/shard_map/reduce_scatter | solution.py:62
  197.2 2.1 copy-start
  199.3 1.4 copy-start.1
  202.4 68.1 %reduce-scatter.8.cloned.1.call-start = ((), (), s32[]{:S(2)}) async-start(), calls=%async_computation.11 | async-start | bytes 1802240 | tf_op jit(solution)/shard_map/reduce_scatter | solution.py:66
  204.1 102.7 %reduce-scatter.6.cloned.1.call-start = ((), (), s32[]{:S(2)}) async-start(), calls=%async_computation.10 | async-start | bytes 1802240 | tf_op jit(solution)/shard_map/reduce_scatter | solution.py:66
Sparse Core Ops, SparseCore 0:
  60.2 28.7 all-gather.4
  91.1 34.4 all-gather.10
  127.7 33.7 all-gather.6
  163.4 33.7 all-gather.8
  202.5 30.1 reduce-scatter.3
  236.3 34.1 reduce-scatter.7
  274.2 32.5 reduce-scatter.5
where the time goes:
time: 314 us
  waiting for transfers between devices  196 us (62%)
  blocking collectives  84.6 us (27%)
  between operations  14.2 us (5%)
  matrix products  12.9 us (4%)
  local copies, waits for them, and re-layouts  3.33 us (1%)
    all_gather x3, waiting for transfers between devices, on_device(): lax.all_gather(w, 'dp', axis=1, tiled=True)[0]  103 us
    all_to_all x1, blocking collectives, on_device(): lax.all_to_all(packed.reshape(owners, CAP, 2 * part), 'expert', split_axi...  49.1 us
    reduce_scatter x2, waiting for transfers between devices, on_device(): lax.psum_scatter(term.astype(jnp.bfloat16), 'dp', scatter_dimension=0, ti...  37.8 us
    all_to_all x1, blocking collectives, on_device(): lax.all_to_all(summed.reshape(owners, CAP, part), 'expert', split_axis=0,...  35.4 us
    reduce_scatter x1, waiting for transfers between devices, on_device(): lax.psum_scatter(partial_value.astype(jnp.bfloat16), 'tensor', scatter_di...  26.9 us
    all_gather x1, waiting for transfers between devices, on_device(): whole = lax.all_gather(arrived, 'tensor', axis=0, tiled=False)  26.8 us
  transfers between devices with their start and end apart: 7, of which 7 were waited for; matrix products, arithmetic and copies ran while one was open for 3% of the time, Pallas kernels for 0%

commit v1 on v0

--- a/solution.py
+++ b/solution.py
@@ -27,7 +27,15 @@
     slot_count = owners * CAP
     placer = bucket_matrix(expert_ids, expert_count, CAP)
     gate_full, down_full, up_full = (
-        lax.all_gather(w, "dp", axis=1, tiled=True)[0]
+        jnp.concatenate(
+            lax.all_to_all(
+                jnp.stack([w for _ in range(lax.psum(1, axis_name="dp"))], 0),
+                axis_name="dp",
+                split_axis=0,
+                concat_axis=0,
+            ),
+            1,
+        )[0]
         for w in (gate_weight, down_weight, up_weight)
     )
     start = lax.axis_index("tensor") * part

time: 314 us -> 241 us (0.77)
  the two profiles are of different devices: /device:TPU:4 before, /device:TPU:2 now
where the time goes in v1:
time: 241 us; the launch traced here: 240 us
  blocking collectives  106 us (44%)
  waiting for transfers between devices  86.6 us (36%)
  between operations  14 us (6%)
  local copies, waits for them, and re-layouts  12.8 us (5%)
  matrix products  9.63 us (4%)
  starting transfers between devices  8.27 us (3%)
  other arithmetic  2.45 us (1%)
    all_to_all x1, blocking collectives, on_device(): lax.all_to_all(packed.reshape(owners, CAP, 2 * part), 'expert', split_axi...  49.1 us
    reduce_scatter x2, waiting for transfers between devices, on_device(): lax.psum_scatter(term.astype(jnp.bfloat16), 'dp', scatter_dimension=0, ti...  38.1 us
    all_to_all x1, blocking collectives, on_device(): lax.all_to_all(summed.reshape(owners, CAP, part), 'expert', split_axis=0,...  35.4 us
    all_to_all x2, waiting for transfers between devices, on_device(): lax.all_to_all(jnp.stack([w for _ in range(lax.psum(1, axis_name='dp'))],...  31.3 us
    all_to_all x1, blocking collectives, on_device(): lax.all_to_all(jnp.stack([w for _ in range(lax.psum(1, axis_name='dp'))],...  21.8 us
    reduce_scatter x1, waiting for transfers between devices, on_device(): lax.psum_scatter(partial_value.astype(jnp.bfloat16), 'tensor', scatter_di...  16.5 us
    all_to_all x2, starting transfers between devices, on_device(): lax.all_to_all(jnp.stack([w for _ in range(lax.psum(1, axis_name='dp'))],...  8.15 us
  transfers between devices with their start and end apart: 6, of which 5 were waited for; matrix products, arithmetic and copies ran while one was open for 5% of the time, Pallas kernels for 0%

profile of v1, /device:TPU:2, one launch (start us, length us, event | category | flops | bytes accessed | tf_op | source)
XLA Modules:
  0.0 240.1 jit_solution(3201230682311457094)
XLA Ops:
  7.2 0.8 fusion.19
  8.0 0.2 reduce_window_sum.11
  8.1 0.8 select_reduce_fusion
  9.0 0.7 multiply_add_fusion
  9.6 1.0 constant_dynamic-slice_fusion
  10.6 0.3 fusion.1
  10.9 49.1 %all_to_all.25 = bf16[32,8,1024]{2,1,0:T(8,128)(2,1)} all-to-all(bf16[32,8,1024]{2,1,0:T(8,128)(2,1)S(1)} %fusion.1), channel_id=1, replica_groups=mesh['dp'=4,'expert'=32,'tensor'=4] {'expert'}, dimensions={0} | all-to-all | bytes 1048576 | tf_op jit(solution)/shard_map/all_to_all | solution.py:46
  60.1 1.2 stack.8
  61.3 4.6 %all-to-all-start.3 = ((bf16[4,1,512,352]{2,3,1,0:T(8,128)(2,1)}), bf16[4,1,512,352]{2,3,1,0:T(8,128)(2,1)S(1)}, u32[]{:S(2)}, u32[]{:S(2)}) async-start(bf16[4,1,512,352]{2,3,1,0:T(8,128)(2,1)} %stack.8), calls=%async_computation.3 | async-start | bytes 2883584 | tf_op jit(solution)/shard_map/all_to_all | solution.py:31
  65.9 0.7 all-gather.2.cloned.1.call-update
  66.6 18.8 %all-to-all-done.3 = bf16[4,1,512,352]{2,3,1,0:T(8,128)(2,1)S(1)} async-done(((bf16[4,1,512,352]{2,3,1,0:T(8,128)(2,1)}), bf16[4,1,512,352]{2,3,1,0:T(8,128)(2,1)S(1)}, u32[]{:S(2)}, u32[]{:S(2)}) %all-to-all-start.3) | async-done | bytes 1441824 | tf_op jit(solution)/shard_map/all_to_all | solution.py:31
  85.4 0.1 stack.6
  85.5 21.8 %all_to_all.26 = bf16[4,1,512,352]{2,3,1,0:T(8,128)(2,1)} all-to-all(bf16[4,1,512,352]{2,3,1,0:T(8,128)(2,1)S(1)} %stack.6), channel_id=1, replica_groups=mesh['dp'=4,'expert'=32,'tensor'=4] {'dp'}, dimensions={0} | all-to-all | bytes 2883584 | tf_op jit(solution)/shard_map/all_to_all | solution.py:31
  107.3 1.2 stack.7
  108.5 3.5 %all-to-all-start.2 = ((bf16[4,1,512,352]{2,3,1,0:T(8,128)(2,1)}), bf16[4,1,512,352]{2,3,1,0:T(8,128)(2,1)S(1)}, u32[]{:S(2)}, u32[]{:S(2)}) async-start(bf16[4,1,512,352]{2,3,1,0:T(8,128)(2,1)} %stack.7), calls=%async_computation.2 | async-start | bytes 2883584 | tf_op jit(solution)/shard_map/all_to_all | solution.py:31
  112.1 0.0 reduce-scatter.4.cloned.1.call-start
  112.1 1.1 copy.14
  113.3 0.4 copy.17
  113.7 1.0 copy-done
  114.6 1.1 copy.12
  115.7 1.5 copy.15
  117.2 12.5 %all-to-all-done.2 = bf16[4,1,512,352]{2,3,1,0:T(8,128)(2,1)S(1)} async-done(((bf16[4,1,512,352]{2,3,1,0:T(8,128)(2,1)}), bf16[4,1,512,352]{2,3,1,0:T(8,128)(2,1)S(1)}, u32[]{:S(2)}, u32[]{:S(2)}) %all-to-all-start.2) | async-done | bytes 1441824 | tf_op jit(solution)/shard_map/all_to_all | solution.py:31
  129.7 1.1 copy.13
  130.9 0.4 copy.16
  131.3 0.0 all-gather.2.cloned.1.call-done
  131.3 1.6 slice_bitcast_fusion.3
  132.9 0.0 copy-start.5
  132.9 0.0 copy-start.7
  133.0 0.6 fusion.22
  133.6 0.9 copy-done.1
  134.5 0.6 multiply_convert_fusion
  135.1 0.6 fusion.4
  135.7 0.7 fusion.23
  136.5 0.0 copy-start.6
  136.5 0.0 copy-start.8
  136.5 1.7 fusion
  138.2 0.0 reduce-scatter.4.cloned.1.call-update
  138.3 0.0 reduce-scatter.8.cloned.1.call-start
  138.3 2.6 %convolution_convert_fusion = bf16[2048,352]{0,1:T(8,128)(2,1)} fusion(bf16[256,352]{0,1:T(8,128)(2,1)} %copy-done.11, bf16[256,512]{1,0:T(8,128)(2,1)S(1)} %get-tuple-element.4, bf16[256,512]{1,0:T(8,128)(2,1)S(1)} %copy-done.6, bf16[256,512]{1,0:T(8,128)(2,1)S(1)} %copy-done.8, bf16[256,512]{1,0:T(8,128)(2,1)S(1)} %get-tuple-element.3), kind=kOutput, calls=%fused_computation | convolution fusion | flops 374013952 | bytes 2670592 | tf_op jit(solution)/shard_map/dot_general | solution.py:69
  140.9 0.0 reduce-scatter.8.cloned.1.call-update
  141.0 0.0 reduce-scatter.6.cloned.1.call-start
  141.0 1.7 convolution_convert_fusion.1
  142.7 0.0 reduce-scatter.6.cloned.1.call-update
  142.7 16.5 %reduce-scatter.4.cloned.1.call-done = bf16[256,512]{1,0:T(8,128)(2,1)} async-done(((bf16[256,2048]{1,0:T(8,128)(2,1)}), bf16[256,512]{1,0:T(8,128)(2,1)}) %reduce-scatter.4.cloned.1.call-update) | async-done | bytes 262160 | tf_op jit(solution)/shard_map/reduce_scatter | solution.py:70
  159.2 35.4 %all_to_all.27 = bf16[32,8,512]{2,1,0:T(8,128)(2,1)S(1)} all-to-all(bf16[32,8,512]{2,1,0:T(8,128)(2,1)} %bitcast.66), channel_id=1, replica_groups=mesh['dp'=4,'expert'=32,'tensor'=4] {'expert'}, dimensions={0} | all-to-all | bytes 524288 | tf_op jit(solution)/shard_map/all_to_all | solution.py:77
  194.5 0.9 convolution_convert_fusion.3
  195.4 2.0 reduce-scatter.8.cloned.1.call-done
  197.4 36.1 %reduce-scatter.6.cloned.1.call-done = bf16[512,352]{0,1:T(8,128)(2,1)} async-done(((bf16[2048,352]{0,1:T(8,128)(2,1)}), bf16[512,352]{0,1:T(8,128)(2,1)}) %reduce-scatter.6.cloned.1.call-update) | async-done | bytes 360464 | tf_op jit(solution)/shard_map/reduce_scatter | solution.py:74
  (19 shorter events, 0.0 us)
Async XLA Ops:
  7.2 52.9 %copy-start.2 = (bf16[1,512,352]{1,2,0:T(8,128)(2,1)S(1)}, bf16[1,512,352]{1,2,0:T(8,128)(2,1)}, u32[]{:S(2)}) copy-start(bf16[1,512,352]{1,2,0:T(8,128)(2,1)} %param.9) | copy-start | bytes 1081348
  61.3 24.1 %copy-start.3 = (bf16[1,512,352]{1,2,0:T(8,128)(2,1)S(1)}, bf16[1,512,352]{1,2,0:T(8,128)(2,1)}, u32[]{:S(2)}) copy-start(bf16[1,512,352]{1,2,0:T(8,128)(2,1)} %param.11) | copy-start | bytes 1081348
  61.3 24.1 %all-to-all-start.3 = ((bf16[4,1,512,352]{2,3,1,0:T(8,128)(2,1)}), bf16[4,1,512,352]{2,3,1,0:T(8,128)(2,1)S(1)}, u32[]{:S(2)}, u32[]{:S(2)}) async-start(bf16[4,1,512,352]{2,3,1,0:T(8,128)(2,1)} %stack.8), calls=%async_computation.3 | async-start | bytes 2883584 | tf_op jit(solution)/shard_map/all_to_all | solution.py:31
  65.9 65.4 %all-gather.2.cloned.1.call-start = ((), (), s32[]{:S(2)}) async-start(), calls=%async_computation.8 | async-start | bytes 2621440 | tf_op jit(solution)/shard_map/all_gather | solution.py:49
  85.4 21.9 %copy-start.4 = (bf16[1,512,352]{1,2,0:T(8,128)(2,1)S(1)}, bf16[1,512,352]{1,2,0:T(8,128)(2,1)}, u32[]{:S(2)}) copy-start(bf16[1,512,352]{1,2,0:T(8,128)(2,1)} %param.10) | copy-start | bytes 1081348
  108.5 21.2 %all-to-all-start.2 = ((bf16[4,1,512,352]{2,3,1,0:T(8,128)(2,1)}), bf16[4,1,512,352]{2,3,1,0:T(8,128)(2,1)S(1)}, u32[]{:S(2)}, u32[]{:S(2)}) async-start(bf16[4,1,512,352]{2,3,1,0:T(8,128)(2,1)} %stack.7), calls=%async_computation.2 | async-start | bytes 2883584 | tf_op jit(solution)/shard_map/all_to_all | solution.py:31
  112.1 47.1 %reduce-scatter.4.cloned.1.call-start = ((), (), s32[]{:S(2)}) async-start(), calls=%async_computation.9 | async-start | bytes 1310720 | tf_op jit(solution)/shard_map/reduce_scatter | solution.py:70
  113.3 1.4 copy-start
  132.9 2.2 copy-start.5
  132.9 2.2 copy-start.7
  133.0 1.5 copy-start.1
  135.1 1.4 copy-start.11
  135.7 0.7 copy-start.9
  136.5 1.8 copy-start.6
  136.5 1.8 copy-start.8
  138.3 2.8 %copy-start.10 = (bf16[256,352]{0,1:T(8,128)(2,1)S(1)}, bf16[256,352]{0,1:T(8,128)(2,1)}, u32[]{:S(2)}) copy-start(bf16[256,352]{0,1:T(8,128)(2,1)} %copy-done.9) | copy-start | bytes 540676
  138.3 59.2 %reduce-scatter.8.cloned.1.call-start = ((), (), s32[]{:S(2)}) async-start(), calls=%async_computation.11 | async-start | bytes 1802240 | tf_op jit(solution)/shard_map/reduce_scatter | solution.py:74
  141.0 92.6 %reduce-scatter.6.cloned.1.call-start = ((), (), s32[]{:S(2)}) async-start(), calls=%async_computation.10 | async-start | bytes 1802240 | tf_op jit(solution)/shard_map/reduce_scatter | solution.py:74
Sparse Core Ops, SparseCore 0:
  68.8 29.3 all-gather.1
  138.4 20.7 reduce-scatter.3
  162.9 34.5 reduce-scatter.7
  201.0 32.5 reduce-scatter.5
